TPU v7x, 256 devices: a whole 4x4x8 slice. The times are simulated.
256 devices in a mesh: row: 16 (over z, y_hi), col: 16 (over x, y_lo, core).
Axes of the slice: x: 4, y: 4 (y_hi: 2, y_lo: 2; y = y_hi * 2 + y_lo), z: 8, core: 2. Of those that a mesh axis runs over, the one named last changes fastest.
Arguments:
- amplitudes: float32 [16, 16, 400, 400], P('row', None, 'col'), may hold values from -6 to 6
- integrals: float32 [64, 64, 400, 400], P('row', None, 'col'), may hold values from -0.015625 to 0.015625
- rest: float32 [16, 16, 64, 64], P('col', None, 'row'), may hold values from -6 to 6
- occ_energy: float32 [16], replicated, may hold values from -2 to -0.5
- vir_energy: float32 [64], replicated, may hold values from 0.5 to 3
Outputs:
- new_amps: float32 [16, 16, 64, 64], P('col', None, 'row')
All inputs are finite; a program needn't handle non-finite values.
Results may differ from a plain program's by a relative error of at most 0.000057.
Values sent between devices are 32-bit elements; how exact they have to be, the bound alone decides.
No kernel may reach another device: no remote copies, remote signals or barrier semaphores. Data moves between devices by JAX's collectives and lax.ppermute only.
A program may use at most 128 MiB of HBM per device.

v0:
```python
import jax
import jax.numpy as jnp
from jax import lax
from jax.sharding import PartitionSpec as P


def on_device(amplitudes, integrals, rest, occ_energy, vir_energy):
    row_index = lax.axis_index("row")
    col_index = lax.axis_index("col")
    a_count = integrals.shape[0]
    b_count = integrals.shape[1]
    integral_slab = integrals.reshape(a_count * b_count, -1)
    occupied = amplitudes.shape[1]
    shard_piece = lax.all_gather(amplitudes, "row", axis=0, tiled=True)
    piece_rows = shard_piece.shape[0]
    flattened = shard_piece.reshape(piece_rows * occupied, -1)
    product = lax.dot_general(
        flattened,
        integral_slab,
        (((1,), (1,)), ((), ())),
        precision=lax.Precision.HIGHEST,
        preferred_element_type=jnp.float32,
    )
    partial_value = product.reshape(piece_rows, occupied, a_count, b_count)
    summed = lax.psum_scatter(partial_value, "col", scatter_dimension=0, tiled=True)
    moved = lax.all_to_all(
        lax.all_to_all(summed, "row", split_axis=3, concat_axis=2, tiled=True),
        "col",
        split_axis=1,
        concat_axis=0,
        tiled=True,
    )
    combined = summed + jnp.transpose(moved, (1, 0, 3, 2))
    i_count = combined.shape[0]
    occ_local = lax.dynamic_slice_in_dim(occ_energy, col_index * i_count, i_count, 0)
    vir_local = lax.dynamic_slice_in_dim(vir_energy, row_index * a_count, a_count, 0)
    denominator = (
        vir_local[None, None, :, None]
        + vir_energy[None, None, None, :]
        - occ_local[:, None, None, None]
        - occ_energy[None, :, None, None]
    )
    return (combined + rest) / denominator


def solution(mesh):
    in_specs = (
        P("row", None, "col", None),
        P("row", None, "col", None),
        P("col", None, "row", None),
        P(),
        P(),
    )
    out_specs = P("col", None, "row", None)
    return jax.shard_map(
        on_device, mesh=mesh, in_specs=in_specs, out_specs=out_specs, check_vma=False
    )
```

profile of v0, /device:TPU:1, one launch (start us, length us, event | category | flops | bytes accessed | tf_op | source)
XLA Modules:
  0.0 327.3 jit_solution(11584524614010061250)
XLA Ops:
  6.5 0.0 all-gather.2.cloned.1.call-start
  6.5 0.7 all-gather.2.cloned.1.call-update
  7.3 0.0 copy-start.1
  7.3 0.0 copy-start.2
  7.3 0.0 copy-start
  7.3 0.0 reduce-scatter.2.cloned.1.call-start
  7.3 189.7 %all-gather.2.cloned.1.call-done = f32[16,16,25,400]{3,1,2,0:T(8,128)} async-done(((f32[1,16,25,400]{3,1,2,0:T(8,128)}), f32[16,16,25,400]{3,1,2,0:T(8,128)}) %all-gather.2.cloned.1.call-update) | async-done | bytes 10240016 | tf_op jit(solution)/shard_map/all_gather | solution.py:14
  197.0 26.4 %fusion.3 = f32[16,16,4,64]{3,1,2,0:T(8,128)} fusion(f32[4,64,25,400]{3,1,2,0:T(8,128)} %param.6, f32[16,16,25,400]{3,1,2,0:T(8,128)} %all-gather.2.cloned.1.call-done), kind=kOutput, calls=%fused_computation.3 | convolution fusion | flops 7864320000 | bytes 20742144 | tf_op jit(solution)/shard_map/dot_general | solution.py:17
  223.4 0.0 reduce-scatter.2.cloned.1.call-update
  223.4 58.5 %reduce-scatter.2.cloned.1.call-done = f32[1,16,4,64]{3,1,2,0:T(8,128)} async-done(((f32[16,16,4,64]{3,1,2,0:T(8,128)}), f32[1,16,4,64]{3,1,2,0:T(8,128)}) %reduce-scatter.2.cloned.1.call-update) | async-done | bytes 16400 | tf_op jit(solution)/shard_map/reduce_scatter | solution.py:25
  281.9 0.9 copy.14
  282.8 0.7 reshape.59
  283.5 9.0 %all-to-all-start = ((f32[16,1,256]{2,1,0:T(1,128)}), f32[16,1,256]{2,1,0:T(1,128)S(1)}, u32[]{:S(2)}, u32[]{:S(2)}) async-start(f32[16,1,256]{2,1,0:T(1,128)} %reshape.59), calls=%async_computation.1 | async-start | bytes 32768 | tf_op jit(solution)/shard_map/all_to_all | solution.py:27
  292.6 0.0 copy-done.1
  292.6 0.6 dynamic_slice.7
  293.2 0.0 copy-done.2
  293.2 0.1 dynamic_slice.6
  293.2 8.2 %all-to-all-done = f32[16,1,256]{2,1,0:T(1,128)S(1)} async-done(((f32[16,1,256]{2,1,0:T(1,128)}), f32[16,1,256]{2,1,0:T(1,128)S(1)}, u32[]{:S(2)}, u32[]{:S(2)}) %all-to-all-start) | async-done | bytes 16416 | tf_op jit(solution)/shard_map/all_to_all | solution.py:27
  301.5 0.6 broadcast.48
  302.1 0.7 reduce
  302.8 0.1 reshape.60
  303.0 0.1 copy.16
  303.1 0.1 copy.17
  303.2 0.7 reshape.61
  303.9 8.4 %all-to-all-start.1 = ((f32[16,1,256]{2,1,0:T(1,128)}), f32[16,1,256]{2,1,0:T(1,128)S(1)}, u32[]{:S(2)}, u32[]{:S(2)}) async-start(f32[16,1,256]{2,1,0:T(1,128)} %reshape.61), calls=%async_computation.2 | async-start | bytes 32768 | tf_op jit(solution)/shard_map/all_to_all | solution.py:26
  312.3 0.6 add_subtract_fusion
  312.9 5.2 %all-to-all-done.1 = f32[16,1,256]{2,1,0:T(1,128)S(1)} async-done(((f32[16,1,256]{2,1,0:T(1,128)}), f32[16,1,256]{2,1,0:T(1,128)S(1)}, u32[]{:S(2)}, u32[]{:S(2)}) %all-to-all-start.1) | async-done | bytes 16416 | tf_op jit(solution)/shard_map/all_to_all | solution.py:26
  318.2 0.7 reduce.1
  318.9 0.1 reshape.62
  319.0 0.0 copy-done
  319.0 0.8 fusion.9
  319.8 0.6 copy.20
  (1 shorter events, 0.0 us)
Async XLA Ops:
  6.5 190.5 %all-gather.2.cloned.1.call-start = ((), (), s32[]{:S(2)}) async-start(), calls=%async_computation.3 | async-start | bytes 13926400 | tf_op jit(solution)/shard_map/all_gather | solution.py:14
  7.3 285.3 %copy-start.1 = (f32[16]{0:T(128)S(1)}, f32[16]{0:T(128)}, u32[]{:S(2)}) copy-start(f32[16]{0:T(128)} %param.8) | copy-start | bytes 196
  7.3 285.9 %copy-start.2 = (f32[64]{0:T(128)S(1)}, f32[64]{0:T(128)}, u32[]{:S(2)}) copy-start(f32[64]{0:T(128)} %param.9) | copy-start | bytes 772
  7.3 311.7 %copy-start = (f32[1,16,4,64]{3,2,1,0:T(4,128)S(1)}, f32[1,16,4,64]{3,2,1,0:T(4,128)}, u32[]{:S(2)}) copy-start(f32[1,16,4,64]{3,2,1,0:T(4,128)} %param.7) | copy-start | bytes 49156
  7.3 274.6 %reduce-scatter.2.cloned.1.call-start = ((), (), s32[]{:S(2)}) async-start(), calls=%async_computation.4 | async-start | bytes 557056 | tf_op jit(solution)/shard_map/reduce_scatter | solution.py:25
  283.5 18.0 %all-to-all-start = ((f32[16,1,256]{2,1,0:T(1,128)}), f32[16,1,256]{2,1,0:T(1,128)S(1)}, u32[]{:S(2)}, u32[]{:S(2)}) async-start(f32[16,1,256]{2,1,0:T(1,128)} %reshape.59), calls=%async_computation.1 | async-start | bytes 32768 | tf_op jit(solution)/shard_map/all_to_all | solution.py:27
  303.9 14.3 %all-to-all-start.1 = ((f32[16,1,256]{2,1,0:T(1,128)}), f32[16,1,256]{2,1,0:T(1,128)S(1)}, u32[]{:S(2)}, u32[]{:S(2)}) async-start(f32[16,1,256]{2,1,0:T(1,128)} %reshape.61), calls=%async_computation.2 | async-start | bytes 32768 | tf_op jit(solution)/shard_map/all_to_all | solution.py:26
Sparse Core Ops, SparseCore 0:
  9.9 187.0 all-gather.1
  223.5 58.3 reduce-scatter.1
where the time goes:
time: 328 us; the launch traced here: 327 us
  waiting for transfers between devices  262 us (80%)
  matrix products  26.4 us (8%)
  starting transfers between devices  17.5 us (5%)
  between operations  13.5 us (4%)
  local copies, waits for them, and re-layouts  4.61 us (1%)
    all_gather x1, waiting for transfers between devices, on_device(): shard_piece = lax.all_gather(amplitudes, 'row', axis=0, tiled=True)  190 us
    reduce_scatter x1, waiting for transfers between devices, on_device(): lax.psum_scatter(partial_value, 'col', scatter_dimension=0, tiled=True)  58.5 us
    dot_general x1, matrix products, on_device(): lax.dot_general(flattened, integral_slab, (((1,), (1,)), ((), ())), preci...  26.4 us
    all_to_all x1, starting transfers between devices, on_device(): lax.all_to_all(summed, 'row', split_axis=3, concat_axis=2, tiled=True)  9.03 us
    all_to_all x1, starting transfers between devices, on_device(): lax.all_to_all(lax.all_to_all(summed, 'row', split_axis=3, concat_axis=2,...  8.43 us
    all_to_all x1, waiting for transfers between devices, on_device(): lax.all_to_all(summed, 'row', split_axis=3, concat_axis=2, tiled=True)  8.25 us
  transfers between devices with their start and end apart: 4, of which 4 were waited for; matrix products, arithmetic and copies ran while one was open for 0% of the time, Pallas kernels for 0%

commit v1 on v0

--- a/solution.py
+++ b/solution.py
@@ -11,7 +11,8 @@
     b_count = integrals.shape[1]
     integral_slab = integrals.reshape(a_count * b_count, -1)
     occupied = amplitudes.shape[1]
-    shard_piece = lax.all_gather(amplitudes, "row", axis=0, tiled=True)
+    outgoing = jnp.stack([amplitudes] * lax.axis_size("row"))
+    shard_piece = jnp.concatenate(lax.all_to_all(outgoing, "row", 0, 0), axis=0)
     piece_rows = shard_piece.shape[0]
     flattened = shard_piece.reshape(piece_rows * occupied, -1)
     product = lax.dot_general(

time: 328 us -> 486 us (1.48)
  local copies, waits for them, and re-layouts: 4.61 us -> 83.5 us
  waiting for transfers between devices: 262 us -> 336 us
  starting transfers between devices: 17.5 us -> 29.3 us
  matrix products: 26.4 us -> 20.9 us
    all_to_all x0 -> x1, waiting for transfers between devices: none -> 261 us  [on_device(): shard_piece = jnp.concatenate(lax.all_to_all(outgoing, 'row', 0, 0), axis=0)]
    all_gather x1 -> x0, waiting for transfers between devices: 190 us -> none  [on_device(): shard_piece = lax.all_gather(amplitudes, 'row', axis=0, tiled=True)]
    dot_general x0 -> x2, local copies, waits for them, and re-layouts: none -> 31.7 us  [on_device(): lax.dot_general(flattened, integral_slab, (((1,), (1,)), ((), ())), preci...]
    all_to_all x0 -> x1, local copies, waits for them, and re-layouts: none -> 21.4 us  [on_device(): shard_piece = jnp.concatenate(lax.all_to_all(outgoing, 'row', 0, 0), axis=0)]
    unnamed x10 -> x11, local copies, waits for them, and re-layouts: 1.69 us -> 20 us
    all_to_all x0 -> x1, starting transfers between devices: none -> 11.8 us  [on_device(): shard_piece = jnp.concatenate(lax.all_to_all(outgoing, 'row', 0, 0), axis=0)]
    another operation x0 -> x1, local copies, waits for them, and re-layouts: none -> 7.51 us  [on_device(): outgoing = jnp.stack([amplitudes] * lax.axis_size('row'))]
    dot_general x1, matrix products: 26.4 us -> 20.9 us  [on_device(): lax.dot_general(flattened, integral_slab, (((1,), (1,)), ((), ())), preci...]
  transfers between devices with their start and end apart: 4 -> 4, of which waited for: 4 -> 4; matrix products, arithmetic and copies ran while one was open for 0% -> 7% of each run, Pallas kernels for 0% -> 0%
where the time goes in v1:
time: 486 us
  waiting for transfers between devices  336 us (69%)
  local copies, waits for them, and re-layouts  83.5 us (17%)
  starting transfers between devices  29.3 us (6%)
  matrix products  20.9 us (4%)
  between operations  13.5 us (3%)
    all_to_all x1, waiting for transfers between devices, on_device(): shard_piece = jnp.concatenate(lax.all_to_all(outgoing, 'row', 0, 0), axis=0)  261 us
    reduce_scatter x1, waiting for transfers between devices, on_device(): lax.psum_scatter(partial_value, 'col', scatter_dimension=0, tiled=True)  61 us
    dot_general x2, local copies, waits for them, and re-layouts, on_device(): lax.dot_general(flattened, integral_slab, (((1,), (1,)), ((), ())), preci...  31.7 us
    all_to_all x1, local copies, waits for them, and re-layouts, on_device(): shard_piece = jnp.concatenate(lax.all_to_all(outgoing, 'row', 0, 0), axis=0)  21.4 us
    dot_general x1, matrix products, on_device(): lax.dot_general(flattened, integral_slab, (((1,), (1,)), ((), ())), preci...  20.9 us
    unnamed x11, local copies, waits for them, and re-layouts  20 us
    all_to_all x1, starting transfers between devices, on_device(): shard_piece = jnp.concatenate(lax.all_to_all(outgoing, 'row', 0, 0), axis=0)  11.8 us
  transfers between devices with their start and end apart: 4, of which 4 were waited for; matrix products, arithmetic and copies ran while one was open for 7% of the time, Pallas kernels for 0%

profile of v1, /device:TPU:1, one launch (start us, length us, event | category | flops | bytes accessed | tf_op | source)
XLA Modules:
  0.0 485.6 jit_solution(8617481606993832290)
XLA Ops:
  6.5 7.5 %stack.2 = f32[16,1,16,25,400]{4,2,3,1,0:T(8,128)} broadcast(f32[16,25,400]{2,0,1:T(8,128)} %bitcast.24), dimensions={2,3,4} | broadcast | bytes 10880000 | tf_op jit(solution)/shard_map/stack | solution.py:14
  14.0 11.8 %all-to-all-start = ((f32[16,1,16,25,400]{4,2,3,1,0:T(8,128)}), f32[16,1,16,25,400]{4,2,3,1,0:T(8,128)}, u32[]{:S(2)}, u32[]{:S(2)}) async-start(f32[16,1,16,25,400]{4,2,3,1,0:T(8,128)} %stack.2), calls=%async_computation | async-start | bytes 26214400 | tf_op jit(solution)/shard_map/all_to_all | solution.py:15
  25.8 0.0 reduce-scatter.2.cloned.1.call-start
  25.9 18.3 %copy.18 = f32[4,64,25,400]{3,2,1,0:T(8,128)} copy(f32[4,64,25,400]{3,1,2,0:T(8,128)} %param.6) | data formatting | bytes 20480000 | tf_op args[1]
  44.2 15.8 %reshape.59 = f32[4,64,10000,1]{2,1,0,3:T(8,128)} reshape(f32[4,64,25,400]{3,2,1,0:T(8,128)} %copy.18) | data formatting | bytes 20480000 | tf_op jit(solution)/shard_map/dot_general | solution.py:18
  60.0 261.4 %all-to-all-done = f32[16,1,16,25,400]{4,2,3,1,0:T(8,128)} async-done(((f32[16,1,16,25,400]{4,2,3,1,0:T(8,128)}), f32[16,1,16,25,400]{4,2,3,1,0:T(8,128)}, u32[]{:S(2)}, u32[]{:S(2)}) %all-to-all-start) | async-done | bytes 10240032 | tf_op jit(solution)/shard_map/all_to_all | solution.py:15
  321.4 21.4 %copy.17 = f32[16,1,16,25,400]{4,3,2,0,1:T(8,128)} copy(f32[16,1,16,25,400]{4,2,3,1,0:T(8,128)} %all-to-all-done) | data formatting | bytes 20480000 | tf_op jit(solution)/shard_map/all_to_all | solution.py:15
  342.8 15.8 %reshape.58 = f32[16,16,10000,1]{2,1,0,3:T(8,128)} reshape(f32[16,1,16,25,400]{4,3,2,0,1:T(8,128)} %copy.17) | data formatting | bytes 20480000 | tf_op jit(solution)/shard_map/dot_general | solution.py:18
  358.7 0.0 copy-start.2
  358.7 0.0 copy-start.1
  358.7 0.0 copy-start
  358.7 20.9 %fusion = f32[16,16,4,64]{3,1,2,0:T(8,128)} fusion(f32[4,64,10000,1]{2,1,0,3:T(8,128)} %reshape.59, f32[16,16,10000,1]{2,1,0,3:T(8,128)} %reshape.58), kind=kOutput, calls=%fused_computation | convolution fusion | flops 7864320000 | bytes 20742144 | tf_op jit(solution)/shard_map/dot_general | solution.py:18
  379.5 0.0 reduce-scatter.2.cloned.1.call-update
  379.6 61.0 %reduce-scatter.2.cloned.1.call-done = f32[1,16,4,64]{3,1,2,0:T(8,128)} async-done(((f32[16,16,4,64]{3,1,2,0:T(8,128)}), f32[1,16,4,64]{3,1,2,0:T(8,128)}) %reduce-scatter.2.cloned.1.call-update) | async-done | bytes 16400 | tf_op jit(solution)/shard_map/reduce_scatter | solution.py:26
  440.5 0.9 copy.19
  441.4 0.7 reshape.62
  442.1 9.0 %all-to-all-start.1 = ((f32[16,1,256]{2,1,0:T(1,128)}), f32[16,1,256]{2,1,0:T(1,128)S(1)}, u32[]{:S(2)}, u32[]{:S(2)}) async-start(f32[16,1,256]{2,1,0:T(1,128)} %reshape.62), calls=%async_computation.2 | async-start | bytes 32768 | tf_op jit(solution)/shard_map/all_to_all | solution.py:28
  451.2 0.0 copy-done.2
  451.2 0.1 dynamic_slice.6
  451.3 0.0 copy-done.1
  451.3 0.7 dynamic_slice.7
  451.9 8.2 %all-to-all-done.1 = f32[16,1,256]{2,1,0:T(1,128)S(1)} async-done(((f32[16,1,256]{2,1,0:T(1,128)}), f32[16,1,256]{2,1,0:T(1,128)S(1)}, u32[]{:S(2)}, u32[]{:S(2)}) %all-to-all-start.1) | async-done | bytes 16416 | tf_op jit(solution)/shard_map/all_to_all | solution.py:28
  460.1 0.5 broadcast.51
  460.6 0.6 reduce
  461.2 0.1 reshape.63
  461.4 0.1 copy.21
  461.5 0.1 copy.22
  461.5 0.7 reshape.64
  462.3 8.4 %all-to-all-start.2 = ((f32[16,1,256]{2,1,0:T(1,128)}), f32[16,1,256]{2,1,0:T(1,128)S(1)}, u32[]{:S(2)}, u32[]{:S(2)}) async-start(f32[16,1,256]{2,1,0:T(1,128)} %reshape.64), calls=%async_computation.3 | async-start | bytes 32768 | tf_op jit(solution)/shard_map/all_to_all | solution.py:27
  470.7 0.8 add_subtract_fusion
  471.4 5.1 %all-to-all-done.2 = f32[16,1,256]{2,1,0:T(1,128)S(1)} async-done(((f32[16,1,256]{2,1,0:T(1,128)}), f32[16,1,256]{2,1,0:T(1,128)S(1)}, u32[]{:S(2)}, u32[]{:S(2)}) %all-to-all-start.2) | async-done | bytes 16416 | tf_op jit(solution)/shard_map/all_to_all | solution.py:27
  476.5 0.6 reduce.1
  477.1 0.1 reshape.65
  477.2 0.0 copy-done
  477.2 0.8 fusion.3
  478.1 0.6 copy.25
  (1 shorter events, 0.0 us)
Async XLA Ops:
  14.0 307.4 %all-to-all-start = ((f32[16,1,16,25,400]{4,2,3,1,0:T(8,128)}), f32[16,1,16,25,400]{4,2,3,1,0:T(8,128)}, u32[]{:S(2)}, u32[]{:S(2)}) async-start(f32[16,1,16,25,400]{4,2,3,1,0:T(8,128)} %stack.2), calls=%async_computation | async-start | bytes 26214400 | tf_op jit(solution)/shard_map/all_to_all | solution.py:15
  25.8 414.7 %reduce-scatter.2.cloned.1.call-start = ((), (), s32[]{:S(2)}) async-start(), calls=%async_computation.4 | async-start | bytes 557056 | tf_op jit(solution)/shard_map/reduce_scatter | solution.py:26
  358.7 92.5 %copy-start.2 = (f32[64]{0:T(128)S(1)}, f32[64]{0:T(128)}, u32[]{:S(2)}) copy-start(f32[64]{0:T(128)} %param.9) | copy-start | bytes 772
  358.7 92.6 %copy-start.1 = (f32[16]{0:T(128)S(1)}, f32[16]{0:T(128)}, u32[]{:S(2)}) copy-start(f32[16]{0:T(128)} %param.8) | copy-start | bytes 196
  358.7 118.6 %copy-start = (f32[1,16,4,64]{3,2,1,0:T(4,128)S(1)}, f32[1,16,4,64]{3,2,1,0:T(4,128)}, u32[]{:S(2)}) copy-start(f32[1,16,4,64]{3,2,1,0:T(4,128)} %param.7) | copy-start | bytes 49156
  442.1 18.0 %all-to-all-start.1 = ((f32[16,1,256]{2,1,0:T(1,128)}), f32[16,1,256]{2,1,0:T(1,128)S(1)}, u32[]{:S(2)}, u32[]{:S(2)}) async-start(f32[16,1,256]{2,1,0:T(1,128)} %reshape.62), calls=%async_computation.2 | async-start | bytes 32768 | tf_op jit(solution)/shard_map/all_to_all | solution.py:28
  462.3 14.3 %all-to-all-start.2 = ((f32[16,1,256]{2,1,0:T(1,128)}), f32[16,1,256]{2,1,0:T(1,128)S(1)}, u32[]{:S(2)}, u32[]{:S(2)}) async-start(f32[16,1,256]{2,1,0:T(1,128)} %reshape.64), calls=%async_computation.3 | async-start | bytes 32768 | tf_op jit(solution)/shard_map/all_to_all | solution.py:27
Sparse Core Ops, SparseCore 0:
  379.7 60.7 reduce-scatter.1
